TPU v7x, 32 devices: a whole 2x2x4 slice. The times are simulated.
32 devices in a mesh: dp: 16 (over z, y, x), ctx: 2 (over core).
Axes of the slice: x: 2, y: 2, z: 4, core: 2. Of those that a mesh axis runs over, the one named last changes fastest.
Arguments:
- layer_in: bfloat16 [16, 256, 4096], P('dp', 'ctx'), may hold values from -6 to 6
- inner_act: bfloat16 [16, 256, 2176], P('dp', 'ctx'), may hold values from -6 to 6
- readout: bfloat16 [16, 256, 64], P('dp', 'ctx'), may hold values from -0.75 to 0.75
- w_in: bfloat16 [4096, 132], P('dp'), may hold values from -0.09375 to 0.09375
- a_log: float32 [68], replicated, may hold values from -3.9 to -1.6
- dt_bias: float32 [68], replicated, may hold values from -4 to -1
- d_skip: float32 [68], replicated, may hold values from 0.5 to 1.5
- grad_out: bfloat16 [16, 256, 2176], P('dp', 'ctx'), may hold values from -6 to 6
Outputs:
- grad_x: bfloat16 [16, 256, 2176], P('dp', 'ctx')
- grad_c: bfloat16 [16, 256, 64], P('dp', 'ctx')
- grad_proj: bfloat16 [16, 256, 132], P('dp', 'ctx')
- grad_w: float32 [4096, 132], P('dp', 'ctx')
All inputs are finite; a program needn't handle non-finite values.
Results may differ from a plain program's by a relative error of at most 0.015.
Values may be sent and summed in bfloat16 or wider, within the bound.
A program may use at most 64 MiB of HBM per device.

v0:
```python
import jax
import jax.numpy as jnp
from jax import lax
from jax.sharding import PartitionSpec as P

STATE = 64
BLOCK = 128


def entering(array, axis, join, neutral, backward):
    count = lax.axis_size(axis)
    place = lax.axis_index(axis)
    ahead = count - 1 - place if backward else place
    gathered = jax.tree.map(
        lambda a, kind: lax.all_gather(a.astype(kind), axis), array, (jnp.bfloat16, jnp.bfloat16)
    )
    state = jax.tree.map(lambda a, e: jnp.zeros_like(a) + jnp.asarray(e, a.dtype), array, neutral)

    def one(turn, state):
        source = count - 1 - turn if backward else turn
        return join(
            state,
            jax.tree.map(
                lambda a, own: lax.dynamic_index_in_dim(a, source, 0, False).astype(own.dtype),
                gathered,
                array,
            ),
        )

    return lax.fori_loop(0, ahead, one, state)


def prepare(projected, a_log, dt_bias):
    b_rows = projected[:, :STATE].astype(jnp.bfloat16)
    step_size = jax.nn.softplus(projected[:, STATE:] + dt_bias)
    decay_rate = -jnp.exp(a_log) * step_size
    return (b_rows, step_size, decay_rate)


def blocked(values, width):
    return values.reshape(values.shape[0] // BLOCK, BLOCK, width)


def split_blocks(projected, inner_rows, a_log, dt_bias):
    row_count = projected.shape[0]
    head_count = a_log.shape[0]
    head_width = inner_rows.shape[1] // head_count
    b_rows, step_size, decay_rate = prepare(projected, a_log, dt_bias)
    inner_blocks = inner_rows.reshape(row_count // BLOCK, BLOCK, head_count, head_width)
    step_blocks = jnp.swapaxes(blocked(step_size, head_count), 1, 2)
    cum_blocks = jnp.cumsum(jnp.swapaxes(blocked(decay_rate, head_count), 1, 2), axis=2)
    return (inner_blocks, blocked(b_rows, STATE), step_blocks, cum_blocks, decay_rate)


def state_input(inner_c, b_c, step_c, cum_c):
    to_end = jnp.exp(cum_c[:, -1:] - cum_c) * step_c
    weighted = (b_c.astype(jnp.float32)[None] * to_end[:, :, None]).astype(jnp.bfloat16)
    return jnp.einsum("shp,hsn->hpn", inner_c, weighted, preferred_element_type=jnp.float32)


def block_forward(projected, inner_rows, c_rows, a_log, dt_bias, d_skip, entry_state):
    row_count = projected.shape[0]
    inner_blocks, b_blocks, step_blocks, cum_blocks, decay_rate = split_blocks(
        projected, inner_rows, a_log, dt_bias
    )
    c_blocks = blocked(c_rows, STATE)
    position = jnp.arange(BLOCK)
    causal = position[:, None] >= position[None, :]

    def block_advance(carried, pieces):
        inner_c, b_c, c_c, step_c, cum_c = pieces
        scores = jnp.dot(c_c, b_c.T, preferred_element_type=jnp.float32)
        spread = cum_c[:, :, None] - cum_c[:, None, :]
        factor = jnp.where(causal, jnp.exp(jnp.where(causal, spread, 0.0)), 0.0)
        mixing = (scores[None] * factor * step_c[:, None, :]).astype(jnp.bfloat16)
        within = jnp.einsum("hts,shp->thp", mixing, inner_c, preferred_element_type=jnp.float32)
        added = state_input(inner_c, b_c, step_c, cum_c)
        carried_in = jnp.einsum(
            "tn,hpn->thp", c_c.astype(jnp.float32), carried, precision=lax.Precision.HIGHEST
        )
        carried_in = carried_in * jnp.exp(cum_c).T[:, :, None]
        result = (within + carried_in + d_skip[None, :, None] * inner_c.astype(jnp.float32)).astype(
            jnp.bfloat16
        )
        carried = jnp.exp(cum_c[:, -1])[:, None, None] * carried + added
        return (carried, result)

    final_state, outputs = lax.scan(
        block_advance, entry_state, (inner_blocks, b_blocks, c_blocks, step_blocks, cum_blocks)
    )
    return (outputs.reshape(row_count, inner_rows.shape[1]), final_state)


def local_summary(projected, inner_rows, a_log, dt_bias):
    inner_blocks, b_blocks, step_blocks, cum_blocks, decay_rate = split_blocks(
        projected, inner_rows, a_log, dt_bias
    )
    head_count = a_log.shape[0]
    head_width = inner_rows.shape[1] // head_count

    def local_advance(carried, pieces):
        inner_c, b_c, step_c, cum_c = pieces
        added = state_input(inner_c, b_c, step_c, cum_c)
        return (jnp.exp(cum_c[:, -1])[:, None, None] * carried + added, None)

    zero_state = jnp.zeros((head_count, head_width, STATE), jnp.float32)
    final_state, unused = lax.scan(
        local_advance, zero_state, (inner_blocks, b_blocks, step_blocks, cum_blocks)
    )
    return (jnp.exp(jnp.sum(decay_rate, axis=0)), final_state)


def entry_weights(projected, c_rows, grad_rows, a_log, dt_bias):
    b_rows, step_size, decay_rate = prepare(projected, a_log, dt_bias)
    row_count = projected.shape[0]
    head_count = a_log.shape[0]
    head_width = grad_rows.shape[1] // head_count
    growth = jnp.exp(jnp.cumsum(decay_rate, axis=0))
    weighted = (c_rows.astype(jnp.float32)[:, None, :] * growth[:, :, None]).astype(jnp.bfloat16)
    return jnp.einsum(
        "thp,thn->hpn",
        grad_rows.reshape(row_count, head_count, head_width),
        weighted,
        preferred_element_type=jnp.float32,
    )


def combine_carry(earlier, later):
    return (earlier[0] * later[0], later[1] + later[0][:, None, None] * earlier[1])


def pass_along(decay_total, summary, backward):
    identity = (jnp.ones_like(decay_total), jnp.zeros_like(summary))
    return entering((decay_total, summary), "ctx", combine_carry, identity, backward)


def per_device(layer_in, inner_act, readout, w_in, a_log, dt_bias, d_skip, grad_out):
    tokens = layer_in[0]
    inner_rows = inner_act[0]
    c_rows = readout[0]
    grad_rows = grad_out[0]
    w_full = lax.all_gather(w_in, "dp", axis=0, tiled=True)
    projected = jnp.dot(tokens, w_full, preferred_element_type=jnp.float32)
    decay_total, own_state = local_summary(projected, inner_rows, a_log, dt_bias)
    entry_part = entry_weights(projected, c_rows, grad_rows, a_log, dt_bias)
    entry_state = pass_along(decay_total, own_state, False)[1]
    exit_grad = pass_along(decay_total, entry_part, True)[1]

    def recompute(proj_val, inner_val, c_val):
        return block_forward(proj_val, inner_val, c_val, a_log, dt_bias, d_skip, entry_state)

    primal, pullback = jax.vjp(recompute, projected, inner_rows, c_rows)
    grad_p, grad_v, grad_r = pullback((grad_rows, exit_grad))
    proj_grad = grad_p.astype(jnp.bfloat16)
    seq_count = lax.axis_size("dp")
    contract = (((0,), (0,)), ((), ()))
    summed = lax.psum_scatter(
        lax.dot_general(tokens, proj_grad, contract, preferred_element_type=jnp.float32),
        "dp",
        scatter_dimension=0,
        tiled=True,
    )
    weight_grad = lax.psum_scatter(summed, "ctx", scatter_dimension=1, tiled=True)
    return (grad_v[None], grad_r[None], proj_grad[None], weight_grad / seq_count)


def solution(mesh):
    in_specs = (
        P("dp", "ctx", None),
        P("dp", "ctx", None),
        P("dp", "ctx", None),
        P("dp", None),
        P(),
        P(),
        P(),
        P("dp", "ctx", None),
    )
    out_specs = (P("dp", "ctx", None), P("dp", "ctx", None), P("dp", "ctx", None), P("dp", "ctx"))
    return jax.shard_map(
        per_device, mesh=mesh, in_specs=in_specs, out_specs=out_specs, check_vma=False
    )
```

profile of v0, /device:TPU:0, one launch (start us, length us, event | category | flops | bytes accessed | tf_op | source)
XLA Modules:
  0.0 213.8 jit_solution(7782846302152594224)
XLA Ops:
  8.0 1.4 copy.64
  9.4 1.1 copy.76
  12.5 56.9 %all-gather.5.cloned.1.call-done = bf16[4096,132]{0,1:T(8,128)(2,1)} async-done(((bf16[256,132]{0,1:T(8,128)(2,1)}), bf16[4096,132]{0,1:T(8,128)(2,1)}) %all-gather.5.cloned.1.call-update) | async-done | bytes 1081360 | tf_op jit(solution)/shard_map/all_gather | solution.py:142
  69.4 1.7 fusion.46
  74.6 2.6 %all-gather = bf16[136,32,64]{2,1,0:T(8,128)(2,1)S(1)} all-gather(bf16[68,32,64]{2,1,0:T(8,128)(2,1)S(1)} %fusion.29), channel_id=2, replica_groups=mesh['dp'=16,'ctx'=2] {'ctx'}, dimensions={0}, use_global_device_ids=true | all-gather | bytes 835584 | tf_op jit(solution)/shard_map/all_gather | solution.py:15
  77.5 2.4 %all-reduce.4 = bf16[136]{0:T(256)(128)(2,1)S(1)} all-reduce(bf16[136]{0:T(256)(128)(2,1)S(1)} %dynamic-update-slice), channel_id=3, replica_groups=mesh['dp'=16,'ctx'=2] {'ctx'}, use_global_device_ids=true, to_apply=%add.4 | all-reduce | flops 136 | bytes 544
  80.5 2.4 %fusion.13 = (f32[68,128]{1,0:T(8,128)}, bf16[128,64]{0,1:T(8,128)(2,1)}) fusion(f32[128,64]{0,1:T(8,128)} %fusion.68, f32[68,128]{1,0:T(8,128)} %copy.69, f32[68,32,64]{2,1,0:T(8,128)S(1)} %get-tuple-element.513, bf16[128,68,32]{0,2,1:T(8,128)(2,1)} %bitcast.174), kind=kOutput, calls=%fused_computation.23 | convolution fusion | flops 38419968 | bytes 1232896 | tf_op jit(solution)/shard_map/transpose(jvp())/while/body/eval_jaxpr/shp,hsn->hpn/dot_general | solution.py:58
  83.6 2.7 %all-gather.2 = bf16[136,32,64]{2,1,0:T(8,128)(2,1)} all-gather(bf16[68,32,64]{2,1,0:T(8,128)(2,1)S(1)} %fusion.28), channel_id=4, replica_groups=mesh['dp'=16,'ctx'=2] {'ctx'}, dimensions={0}, use_global_device_ids=true | all-gather | bytes 835584 | tf_op jit(solution)/shard_map/all_gather | solution.py:15
  87.7 1.3 fusion.27
  89.9 0.9 copy.78
  92.7 1.5 copy.80
  94.2 1.6 copy.70
  95.7 6.0 %fusion.11 = (f32[68,128]{1,0:T(8,128)}, f32[68,128]{1,0:T(8,128)}, f32[68,128]{1,0:T(8,128)}, bf16[128,128]{1,0:T(8,128)(2,1)}) fusion(f32[68,128]{1,0:T(8,128)} %copy.73, f32[68,128]{1,0:T(8,128)} %bitcast.177, f32[128,128]{1,0:T(8,128)} %copy.70, pred[128,128]{1,0:T(8,128)(4,1)} %iota_compare_fusion, bf16[68,32,128]{2,1,0:T(8,128)(2,1)} %bitcast.164, ...), kind=kOutput, calls=%fused_computation.19 | convolution fusion | flops 90200576 | bytes 1402880 | tf_op jit(solution)/shard_map/transpose(jvp())/while/body/eval_jaxpr/hts,shp->thp/dot_general | solution.py:76
  101.7 1.5 copy.82
  103.2 1.5 copy.83
  104.7 1.6 fusion.57
  106.2 0.9 copy.84
  107.2 1.9 reduce_window_sum.37
  109.0 1.5 copy.85
  110.5 1.5 copy.79
  112.0 1.4 copy.86
  113.4 1.0 fusion.50
  114.4 1.0 fusion.41
  115.4 1.9 convolution_bitcast_fusion
  118.2 1.1 bitcast_multiply_fusion.2
  119.4 2.0 fusion.42
  121.4 1.5 fusion.44
  123.0 2.0 fusion.30
  125.5 72.9 %reduce-scatter.4.cloned.1.call-done = f32[256,132]{0,1:T(8,128)} async-done(((f32[4096,132]{0,1:T(8,128)}), f32[256,132]{0,1:T(8,128)}) %reduce-scatter.4.cloned.1.call-update) | async-done | bytes 135184 | tf_op jit(solution)/shard_map/reduce_scatter | solution.py:157
  198.4 3.6 %fusion = f32[256,72]{0,1:T(8,128)S(1)} fusion(f32[256,132]{0,1:T(8,128)} %reduce-scatter.4.cloned.1.call-done), kind=kCustom, calls=%all-reduce-scatter | all-reduce-scatter fusion | flops 36865 | bytes 209408
  202.0 2.3 %collective-permute-start = (f32[256,6]{0,1:T(8,128)S(1)}, f32[256,6]{0,1:T(8,128)S(1)}, u32[]{:S(2)}, u32[]{:S(2)}) collective-permute-start(f32[256,6]{0,1:T(8,128)S(1)} %slice.28), channel_id=1, source_target_pairs={{0,1},{2,3},{4,5},{6,7},{8,9},{10,11},{12,13},{14,15},{16,17},{18,... | collective-permute-start | bytes 18440
  205.1 1.1 copy.88
  (101 shorter events, 13.7 us)
Async XLA Ops:
  7.2 62.2 %copy-start = (bf16[1,128,4096]{2,1,0:T(8,128)(2,1)S(1)}, bf16[1,128,4096]{2,1,0:T(8,128)(2,1)}, u32[]{:S(2)}) copy-start(bf16[1,128,4096]{2,1,0:T(8,128)(2,1)} %param.12) | copy-start | bytes 3145732
  7.2 2.2 %copy-start.4 = (bf16[1,128,2176]{2,1,0:T(8,128)(2,1)S(1)}, bf16[1,128,2176]{2,1,0:T(8,128)(2,1)}, u32[]{:S(2)}) copy-start(bf16[1,128,2176]{2,1,0:T(8,128)(2,1)} %param.13) | copy-start | bytes 1671172
  7.2 62.2 %all-gather.5.cloned.1.call-start = ((), (), s32[]{:S(2)}) async-start(), calls=%async_computation.1 | async-start | bytes 1183744 | tf_op jit(solution)/shard_map/all_gather | solution.py:142
  7.9 190.4 %reduce-scatter.4.cloned.1.call-start = ((), (), s32[]{:S(2)}) async-start(), calls=%async_computation.2 | async-start | bytes 2367488 | tf_op jit(solution)/shard_map/reduce_scatter | solution.py:157
  8.0 2.5 %copy-start.24 = (u32[32]{0:T(128)S(1)}, u32[32]{0:T(128)}, u32[]{:S(2)}) copy-start(u32[32]{0:T(128)} %constant.223) | copy-start | bytes 388
  8.0 4.4 %copy-start.26 = (f32[68]{0:T(128)S(1)}, f32[68]{0:T(128)}, u32[]{:S(2)}) copy-start(f32[68]{0:T(128)} %param.16) | copy-start | bytes 820
  8.0 4.4 %copy-start.7 = (bf16[1,128,64]{1,2,0:T(8,128)(2,1)S(1)}, bf16[1,128,64]{1,2,0:T(8,128)(2,1)}, u32[]{:S(2)}) copy-start(bf16[1,128,64]{1,2,0:T(8,128)(2,1)} %param.14) | copy-start | bytes 49156
  9.4 64.6 %copy-start.1 = (bf16[1,128,2176]{1,2,0:T(8,128)(2,1)}, bf16[1,128,2176]{1,2,0:T(8,128)(2,1)S(1)}, u32[]{:S(2)}) copy-start(bf16[1,128,2176]{1,2,0:T(8,128)(2,1)S(1)} %copy.64) | copy-start | bytes 1671172
  12.4 59.4 %copy-start.23 = (f32[68]{0:T(128)}, f32[68]{0:T(128)S(1)}, u32[]{:S(2)}) copy-start(f32[68]{0:T(128)S(1)} %exponential_negate_fusion) | copy-start | bytes 820
  12.4 59.4 %copy-start.22 = (f32[68]{0:T(128)S(1)}, f32[68]{0:T(128)}, u32[]{:S(2)}) copy-start(f32[68]{0:T(128)} %param.17) | copy-start | bytes 820
  71.1 18.0 %copy-start.6 = (f32[128,132]{0,1:T(8,128)}, f32[128,132]{0,1:T(8,128)S(1)}, u32[]{:S(2)}) copy-start(f32[128,132]{0,1:T(8,128)S(1)} %fusion.46) | copy-start | bytes 202756
  72.3 0.6 copy-start.11
  72.9 18.6 %copy-start.21 = (f32[68]{0:T(128)}, f32[68]{0:T(128)S(1)}, u32[]{:S(2)}) copy-start(f32[68]{0:T(128)S(1)} %slice_bitcast_fusion) | copy-start | bytes 820
  80.5 2.4 %copy-start.5 = (bf16[1,128,2176]{1,2,0:T(8,128)(2,1)S(1)}, bf16[1,128,2176]{1,2,0:T(8,128)(2,1)}, u32[]{:S(2)}) copy-start(bf16[1,128,2176]{1,2,0:T(8,128)(2,1)} %copy.76) | copy-start | bytes 1671172
  80.5 2.4 %copy-start.13 = (f32[68,128]{1,0:T(8,128)S(1)}, f32[68,128]{1,0:T(8,128)}, u32[]{:S(2)}) copy-start(f32[68,128]{1,0:T(8,128)} %copy.69) | copy-start | bytes 104452
  80.5 2.4 %copy-start.15 = (f32[128,64]{0,1:T(8,128)S(1)}, f32[128,64]{0,1:T(8,128)}, u32[]{:S(2)}) copy-start(f32[128,64]{0,1:T(8,128)} %fusion.68) | copy-start | bytes 98308
  86.7 1.1 copy-start.2
  86.7 1.0 copy-start.8
  101.7 12.7 %copy-start.9 = (bf16[1,128,64]{1,2,0:T(8,128)(2,1)S(1)}, bf16[1,128,64]{1,2,0:T(8,128)(2,1)}, u32[]{:S(2)}) copy-start(bf16[1,128,64]{1,2,0:T(8,128)(2,1)} %param.14) | copy-start | bytes 49156
  117.3 0.8 copy-start.10
  119.4 2.0 copy-start.17
  119.4 3.6 %copy-start.3 = (bf16[1,128,2176]{1,2,0:T(8,128)(2,1)S(1)}, bf16[1,128,2176]{1,2,0:T(8,128)(2,1)}, u32[]{:S(2)}) copy-start(bf16[1,128,2176]{1,2,0:T(8,128)(2,1)} %copy-done.1) | copy-start | bytes 1671172
  119.4 3.5 %copy-start.12 = (f32[1,68,128]{2,1,0:T(8,128)S(1)}, f32[1,68,128]{2,1,0:T(8,128)}, u32[]{:S(2)}) copy-start(f32[1,68,128]{2,1,0:T(8,128)} %copy-done.11) | copy-start | bytes 104452
  119.4 3.5 %copy-start.18 = (f32[128,128]{1,0:T(8,128)S(1)}, f32[128,128]{1,0:T(8,128)}, u32[]{:S(2)}) copy-start(f32[128,128]{1,0:T(8,128)} %copy.70) | copy-start | bytes 196612
  119.4 3.5 %copy-start.19 = (f32[68,128]{1,0:T(8,128)S(1)}, f32[68,128]{1,0:T(8,128)}, u32[]{:S(2)}) copy-start(f32[68,128]{1,0:T(8,128)} %copy.73) | copy-start | bytes 104452
  119.4 3.5 %copy-start.20 = (pred[128,128]{1,0:T(8,128)(4,1)S(1)}, pred[128,128]{1,0:T(8,128)(4,1)}, u32[]{:S(2)}) copy-start(pred[128,128]{1,0:T(8,128)(4,1)} %iota_compare_fusion) | copy-start | bytes 49156
  123.0 2.0 copy-start.14
  123.0 2.0 copy-start.16
  123.0 2.0 copy-start.25
  202.0 4.1 %collective-permute-start = (f32[256,6]{0,1:T(8,128)S(1)}, f32[256,6]{0,1:T(8,128)S(1)}, u32[]{:S(2)}, u32[]{:S(2)}) collective-permute-start(f32[256,6]{0,1:T(8,128)S(1)} %slice.28), channel_id=1, source_target_pairs={{0,1},{2,3},{4,5},{6,7},{8,9},{10,11},{12,13},{14,15},{16,17},{18,... | collective-permute-start | bytes 18440
Sparse Core Ops, SparseCore 0:
  10.7 58.5 all-gather.4
  117.5 80.8 reduce-scatter.3
where the time goes:
time: 215 us; the launch traced here: 214 us
  waiting for transfers between devices  130 us (60%)
  matrix products  22.4 us (10%)
  local copies, waits for them, and re-layouts  20.8 us (10%)
  between operations  15.9 us (7%)
  blocking collectives  11.4 us (5%)
  other arithmetic  10.2 us (5%)
  starting transfers between devices  2.33 us (1%)
    reduce_scatter x1, waiting for transfers between devices, per_device(): lax.psum_scatter(lax.dot_general(tokens, proj_grad, contract, preferred_e...  72.9 us
    all_gather x1, waiting for transfers between devices, per_device(): w_full = lax.all_gather(w_in, 'dp', axis=0, tiled=True)  56.9 us
    dot_general x2, matrix products, block_advance(): jnp.einsum('hts,shp->thp', mixing, inner_c, preferred_element_type=jnp.fl...  7.92 us
    unnamed x64, local copies, waits for them, and re-layouts  6.5 us
    unnamed x2, blocking collectives  6.08 us
    all_gather x2, blocking collectives, entering(): lax.all_gather(a.astype(kind), axis)  5.35 us
  transfers between devices with their start and end apart: 3, of which 2 were waited for; matrix products, arithmetic and copies ran while one was open for 6% of the time, Pallas kernels for 0%

commit v1 on v0

--- a/solution.py
+++ b/solution.py
@@ -2,6 +2,7 @@
 import jax.numpy as jnp
 from jax import lax
 from jax.sharding import PartitionSpec as P
+from jax.lax import axis_index, ppermute, psum
 
 STATE = 64
 BLOCK = 128
@@ -139,7 +140,25 @@
     inner_rows = inner_act[0]
     c_rows = readout[0]
     grad_rows = grad_out[0]
-    w_full = lax.all_gather(w_in, "dp", axis=0, tiled=True)
+    big = psum(1, "dp")
+    mixed_arr = axis_index("dp")
+    n_now, x_next, small = (big, mixed_arr, w_in.shape[0])
+    rows = tuple((h * n_now if idx == 0 else h for idx, h in enumerate(w_in.shape)))
+    piece_out = jnp.zeros(rows, w_in.dtype)
+    w_full = lax.dynamic_update_slice_in_dim(piece_out, w_in, x_next * small, axis=0)
+    raw_out = moved = w_in
+    for k0 in range(1, n_now // 2 + 1):
+        block_out = tuple(((idx, (idx + 1) % n_now) for idx in range(n_now)))
+        raw_out = ppermute(raw_out, "dp", block_out)
+        w_full = lax.dynamic_update_slice_in_dim(
+            w_full, raw_out, (x_next - k0) % n_now * small, axis=0
+        )
+        if 2 * k0 < n_now:
+            reply = tuple(((idx, (idx - 1) % n_now) for idx in range(n_now)))
+            moved = ppermute(moved, "dp", reply)
+            w_full = lax.dynamic_update_slice_in_dim(
+                w_full, moved, (x_next + k0) % n_now * small, axis=0
+            )
     projected = jnp.dot(tokens, w_full, preferred_element_type=jnp.float32)
     decay_total, own_state = local_summary(projected, inner_rows, a_log, dt_bias)
     entry_part = entry_weights(projected, c_rows, grad_rows, a_log, dt_bias)

time: 215 us -> 223 us (1.037)
  starting transfers between devices: 2.33 us -> 43.3 us
  waiting for transfers between devices: 130 us -> 90.9 us
  other arithmetic: 10.2 us -> 14.2 us
  local copies, waits for them, and re-layouts: 20.8 us -> 23.9 us
    all_gather x1 -> x0, waiting for transfers between devices: 56.9 us -> none  [per_device(): w_full = lax.all_gather(w_in, 'dp', axis=0, tiled=True)]
    ppermute x0 -> x15, starting transfers between devices: none -> 41 us  [the longest x7 38 us: per_device(): moved = ppermute(moved, 'dp', reply)]
    ppermute x0 -> x15, waiting for transfers between devices: none -> 21.7 us  [the longest x8 21.7 us: per_device(): raw_out = ppermute(raw_out, 'dp', block_out)]
    reduce_scatter x1, waiting for transfers between devices: 72.9 us -> 69.1 us  [per_device(): lax.psum_scatter(lax.dot_general(tokens, proj_grad, contract, preferred_e...]
    unnamed x64 -> x63, local copies, waits for them, and re-layouts: 6.5 us -> 7.28 us
  transfers between devices with their start and end apart: 3 -> 17, of which waited for: 2 -> 8; matrix products, arithmetic and copies ran while one was open for 6% -> 6% of each run, Pallas kernels for 0% -> 0%
where the time goes in v1:
time: 223 us; the launch traced here: 222 us
  waiting for transfers between devices  90.9 us (41%)
  starting transfers between devices  43.3 us (19%)
  local copies, waits for them, and re-layouts  23.9 us (11%)
  matrix products  21.4 us (10%)
  between operations  16 us (7%)
  other arithmetic  14.2 us (6%)
  blocking collectives  12.1 us (5%)
    reduce_scatter x1, waiting for transfers between devices, per_device(): lax.psum_scatter(lax.dot_general(tokens, proj_grad, contract, preferred_e...  69.1 us
    ppermute x7, starting transfers between devices, per_device(): moved = ppermute(moved, 'dp', reply)  38 us
    ppermute x8, waiting for transfers between devices, per_device(): raw_out = ppermute(raw_out, 'dp', block_out)  21.7 us
    dot_general x2, matrix products, block_advance(): jnp.einsum('hts,shp->thp', mixing, inner_c, preferred_element_type=jnp.fl...  8.01 us
    unnamed x63, local copies, waits for them, and re-layouts  7.28 us
    unnamed x2, blocking collectives  6.08 us
    all_gather x2, blocking collectives, entering(): lax.all_gather(a.astype(kind), axis)  6.06 us
  transfers between devices with their start and end apart: 17, of which 8 were waited for; matrix products, arithmetic and copies ran while one was open for 6% of the time, Pallas kernels for 0%

profile of v1, /device:TPU:0, one launch (start us, length us, event | category | flops | bytes accessed | tf_op | source)
XLA Modules:
  0.0 222.1 jit_solution(11751471999530494873)
XLA Ops:
  7.2 3.0 %collective-permute-start = (bf16[256,132]{0,1:T(8,128)(2,1)}, bf16[256,132]{0,1:T(8,128)(2,1)S(1)}, u32[]{:S(2)}, u32[]{:S(2)}) collective-permute-start(bf16[256,132]{0,1:T(8,128)(2,1)} %param.15), channel_id=1, source_target_pairs={{0,2},{2,4},{4,6},{6,8},{8,10},{10,12},{12,14},{14,16},{16,18},{18... | collective-permute-start | bytes 202760 | tf_op jit(solution)/shard_map/ppermute | solution.py:152
  10.2 4.1 %collective-permute-start.1 = (bf16[256,132]{0,1:T(8,128)(2,1)}, bf16[256,132]{0,1:T(8,128)(2,1)S(1)}, u32[]{:S(2)}, u32[]{:S(2)}) collective-permute-start(bf16[256,132]{0,1:T(8,128)(2,1)} %param.15), channel_id=1, source_target_pairs={{0,30},{2,0},{4,2},{6,4},{8,6},{10,8},{12,10},{14,12},{16,14},{18,... | collective-permute-start | bytes 202760 | tf_op jit(solution)/shard_map/ppermute | solution.py:158
  20.2 5.6 %collective-permute-start.3 = (bf16[256,132]{0,1:T(8,128)(2,1)S(1)}, bf16[256,132]{0,1:T(8,128)(2,1)S(1)}, u32[]{:S(2)}, u32[]{:S(2)}) collective-permute-start(bf16[256,132]{0,1:T(8,128)(2,1)S(1)} %collective-permute-done.1), channel_id=1, source_target_pairs={{0,30},{2,0},{4,2},{6,4},{8,6},{10,8},{12,10},{14,12},{16,14},{18,... | collective-permute-start | bytes 202760 | tf_op jit(solution)/shard_map/ppermute | solution.py:158
  25.8 2.4 %collective-permute-done.2 = bf16[256,132]{0,1:T(8,128)(2,1)S(1)} collective-permute-done((bf16[256,132]{0,1:T(8,128)(2,1)S(1)}, bf16[256,132]{0,1:T(8,128)(2,1)S(1)}, u32[]{:S(2)}, u32[]{:S(2)}) %collective-permute-start.2) | collective-permute-done | bytes 67616 | tf_op jit(solution)/shard_map/ppermute | solution.py:152
  28.2 5.6 %collective-permute-start.5 = (bf16[256,132]{0,1:T(8,128)(2,1)S(1)}, bf16[256,132]{0,1:T(8,128)(2,1)S(1)}, u32[]{:S(2)}, u32[]{:S(2)}) collective-permute-start(bf16[256,132]{0,1:T(8,128)(2,1)S(1)} %collective-permute-done.3), channel_id=1, source_target_pairs={{0,30},{2,0},{4,2},{6,4},{8,6},{10,8},{12,10},{14,12},{16,14},{18,... | collective-permute-start | bytes 202760 | tf_op jit(solution)/shard_map/ppermute | solution.py:158
  33.8 2.2 %collective-permute-done.4 = bf16[256,132]{0,1:T(8,128)(2,1)S(1)} collective-permute-done((bf16[256,132]{0,1:T(8,128)(2,1)S(1)}, bf16[256,132]{0,1:T(8,128)(2,1)S(1)}, u32[]{:S(2)}, u32[]{:S(2)}) %collective-permute-start.4) | collective-permute-done | bytes 67616 | tf_op jit(solution)/shard_map/ppermute | solution.py:152
  36.1 5.6 %collective-permute-start.7 = (bf16[256,132]{0,1:T(8,128)(2,1)S(1)}, bf16[256,132]{0,1:T(8,128)(2,1)S(1)}, u32[]{:S(2)}, u32[]{:S(2)}) collective-permute-start(bf16[256,132]{0,1:T(8,128)(2,1)S(1)} %collective-permute-done.5), channel_id=1, source_target_pairs={{0,30},{2,0},{4,2},{6,4},{8,6},{10,8},{12,10},{14,12},{16,14},{18,... | collective-permute-start | bytes 202760 | tf_op jit(solution)/shard_map/ppermute | solution.py:158
  41.7 2.4 %collective-permute-done.6 = bf16[256,132]{0,1:T(8,128)(2,1)S(1)} collective-permute-done((bf16[256,132]{0,1:T(8,128)(2,1)S(1)}, bf16[256,132]{0,1:T(8,128)(2,1)S(1)}, u32[]{:S(2)}, u32[]{:S(2)}) %collective-permute-start.6) | collective-permute-done | bytes 67616 | tf_op jit(solution)/shard_map/ppermute | solution.py:152
  44.1 5.6 %collective-permute-start.9 = (bf16[256,132]{0,1:T(8,128)(2,1)S(1)}, bf16[256,132]{0,1:T(8,128)(2,1)S(1)}, u32[]{:S(2)}, u32[]{:S(2)}) collective-permute-start(bf16[256,132]{0,1:T(8,128)(2,1)S(1)} %collective-permute-done.7), channel_id=1, source_target_pairs={{0,30},{2,0},{4,2},{6,4},{8,6},{10,8},{12,10},{14,12},{16,14},{18,... | collective-permute-start | bytes 202760 | tf_op jit(solution)/shard_map/ppermute | solution.py:158
  49.7 2.2 %collective-permute-done.8 = bf16[256,132]{0,1:T(8,128)(2,1)S(1)} collective-permute-done((bf16[256,132]{0,1:T(8,128)(2,1)S(1)}, bf16[256,132]{0,1:T(8,128)(2,1)S(1)}, u32[]{:S(2)}, u32[]{:S(2)}) %collective-permute-start.8) | collective-permute-done | bytes 67616 | tf_op jit(solution)/shard_map/ppermute | solution.py:152
  52.0 5.7 %collective-permute-start.11 = (bf16[256,132]{0,1:T(8,128)(2,1)S(1)}, bf16[256,132]{0,1:T(8,128)(2,1)S(1)}, u32[]{:S(2)}, u32[]{:S(2)}) collective-permute-start(bf16[256,132]{0,1:T(8,128)(2,1)S(1)} %collective-permute-done.9), channel_id=1, source_target_pairs={{0,30},{2,0},{4,2},{6,4},{8,6},{10,8},{12,10},{14,12},{16,14},{18,... | collective-permute-start | bytes 202760 | tf_op jit(solution)/shard_map/ppermute | solution.py:158
  57.7 2.4 %collective-permute-done.10 = bf16[256,132]{0,1:T(8,128)(2,1)S(1)} collective-permute-done((bf16[256,132]{0,1:T(8,128)(2,1)S(1)}, bf16[256,132]{0,1:T(8,128)(2,1)S(1)}, u32[]{:S(2)}, u32[]{:S(2)}) %collective-permute-start.10) | collective-permute-done | bytes 67616 | tf_op jit(solution)/shard_map/ppermute | solution.py:152
  60.1 5.8 %collective-permute-start.13 = (bf16[256,132]{0,1:T(8,128)(2,1)S(1)}, bf16[256,132]{0,1:T(8,128)(2,1)S(1)}, u32[]{:S(2)}, u32[]{:S(2)}) collective-permute-start(bf16[256,132]{0,1:T(8,128)(2,1)S(1)} %collective-permute-done.11), channel_id=1, source_target_pairs={{0,30},{2,0},{4,2},{6,4},{8,6},{10,8},{12,10},{14,12},{16,14},{18,... | collective-permute-start | bytes 202760 | tf_op jit(solution)/shard_map/ppermute | solution.py:158
  65.9 2.2 %collective-permute-done.12 = bf16[256,132]{0,1:T(8,128)(2,1)S(1)} collective-permute-done((bf16[256,132]{0,1:T(8,128)(2,1)S(1)}, bf16[256,132]{0,1:T(8,128)(2,1)S(1)}, u32[]{:S(2)}, u32[]{:S(2)}) %collective-permute-start.12) | collective-permute-done | bytes 67616 | tf_op jit(solution)/shard_map/ppermute | solution.py:152
  68.2 7.9 %collective-permute-done.14 = bf16[256,132]{0,1:T(8,128)(2,1)S(1)} collective-permute-done((bf16[256,132]{0,1:T(8,128)(2,1)S(1)}, bf16[256,132]{0,1:T(8,128)(2,1)S(1)}, u32[]{:S(2)}, u32[]{:S(2)}) %collective-permute-start.14) | collective-permute-done | bytes 67616 | tf_op jit(solution)/shard_map/ppermute | solution.py:152
  80.2 2.6 %all-gather.2 = bf16[136,32,64]{2,1,0:T(8,128)(2,1)S(1)} all-gather(bf16[68,32,64]{2,1,0:T(8,128)(2,1)S(1)} %fusion.28), channel_id=4, replica_groups=mesh['dp'=16,'ctx'=2] {'ctx'}, dimensions={0}, use_global_device_ids=true | all-gather | bytes 835584 | tf_op jit(solution)/shard_map/all_gather | solution.py:16
  83.0 2.4 %all-reduce.4 = bf16[136]{0:T(256)(128)(2,1)S(1)} all-reduce(bf16[136]{0:T(256)(128)(2,1)S(1)} %dynamic-update-slice), channel_id=3, replica_groups=mesh['dp'=16,'ctx'=2] {'ctx'}, use_global_device_ids=true, to_apply=%add.4 | all-reduce | flops 136 | bytes 544
  86.5 1.8 fusion.29
  88.3 3.5 %all-gather = bf16[136,32,64]{2,1,0:T(8,128)(2,1)} all-gather(bf16[68,32,64]{2,1,0:T(8,128)(2,1)S(1)} %fusion.29), channel_id=2, replica_groups=mesh['dp'=16,'ctx'=2] {'ctx'}, dimensions={0}, use_global_device_ids=true | all-gather | bytes 835584 | tf_op jit(solution)/shard_map/all_gather | solution.py:16
  91.9 1.5 while.20
  93.5 2.3 %fusion.13 = (f32[68,128]{1,0:T(8,128)}, bf16[128,64]{0,1:T(8,128)(2,1)}) fusion(f32[128,64]{0,1:T(8,128)} %copy-done.14, f32[68,128]{1,0:T(8,128)S(1)} %copy-done.12, f32[68,32,64]{2,1,0:T(8,128)S(1)} %get-tuple-element.513, bf16[128,68,32]{0,2,1:T(8,128)(2,1)} %bitcast.179), kind=kOutput, calls=%fused_computation.23 | convolution fusion | flops 38419968 | bytes 1232896 | tf_op jit(solution)/shard_map/transpose(jvp())/while/body/eval_jaxpr/shp,hsn->hpn/dot_general | solution.py:59
  103.1 1.5 copy.75
  104.7 1.6 copy.72
  106.2 6.0 %fusion.11 = (f32[68,128]{1,0:T(8,128)}, f32[68,128]{1,0:T(8,128)}, f32[68,128]{1,0:T(8,128)}, bf16[128,128]{1,0:T(8,128)(2,1)}) fusion(f32[68,128]{1,0:T(8,128)} %copy.75, f32[68,128]{1,0:T(8,128)} %bitcast.181, f32[128,128]{1,0:T(8,128)} %copy.72, pred[128,128]{1,0:T(8,128)(4,1)} %iota_compare_fusion, bf16[68,32,128]{2,1,0:T(8,128)(2,1)} %bitcast.168, ...), kind=kOutput, calls=%fused_computation.19 | convolution fusion | flops 90200576 | bytes 1402880 | tf_op jit(solution)/shard_map/transpose(jvp())/while/body/eval_jaxpr/hts,shp->thp/dot_general | solution.py:77
  115.2 1.7 fusion.56
  118.5 2.6 %reduce_window_sum.37 = f32[1,68,128]{2,1,0:T(8,128)} reduce-window(f32[1,68,128]{2,1,0:T(8,128)} %copy.86, f32[]{:T(128)} %constant.290.clone.1), window={size=1x1x128 pad=0_0x0_0x0_127}, to_apply=%region_15.16 | reduce-window | flops 1105408 | bytes 69636 | tf_op jit(solution)/shard_map/transpose(jvp(jit(cumsum)))/reduce_window_sum | solution.py:52
  127.5 1.9 convolution_bitcast_fusion
  132.2 2.0 fusion.42
  135.0 2.0 fusion.30
  137.5 69.1 %reduce-scatter.4.cloned.1.call-done = f32[256,132]{0,1:T(8,128)} async-done(((f32[4096,132]{0,1:T(8,128)}), f32[256,132]{0,1:T(8,128)}) %reduce-scatter.4.cloned.1.call-update) | async-done | bytes 135184 | tf_op jit(solution)/shard_map/reduce_scatter | solution.py:176
  206.7 3.6 %fusion = f32[256,72]{0,1:T(8,128)S(1)} fusion(f32[256,132]{0,1:T(8,128)} %reduce-scatter.4.cloned.1.call-done), kind=kCustom, calls=%all-reduce-scatter | all-reduce-scatter fusion | flops 36865 | bytes 209408
  210.3 2.3 %collective-permute-start.15 = (f32[256,6]{0,1:T(8,128)S(1)}, f32[256,6]{0,1:T(8,128)S(1)}, u32[]{:S(2)}, u32[]{:S(2)}) collective-permute-start(f32[256,6]{0,1:T(8,128)S(1)} %slice.28), channel_id=1, source_target_pairs={{0,1},{2,3},{4,5},{6,7},{8,9},{10,11},{12,13},{14,15},{16,17},{18,... | collective-permute-start | bytes 18440
  (144 shorter events, 36.3 us)
Async XLA Ops:
  7.2 68.9 %copy-start = (bf16[1,128,4096]{2,1,0:T(8,128)(2,1)S(1)}, bf16[1,128,4096]{2,1,0:T(8,128)(2,1)}, u32[]{:S(2)}) copy-start(bf16[1,128,4096]{2,1,0:T(8,128)(2,1)} %param.12) | copy-start | bytes 3145732
  7.2 9.2 %copy-start.5 = (bf16[1,128,2176]{2,1,0:T(8,128)(2,1)S(1)}, bf16[1,128,2176]{2,1,0:T(8,128)(2,1)}, u32[]{:S(2)}) copy-start(bf16[1,128,2176]{2,1,0:T(8,128)(2,1)} %param.19) | copy-start | bytes 1671172
  7.2 199.5 %reduce-scatter.4.cloned.1.call-start = ((), (), s32[]{:S(2)}) async-start(), calls=%async_computation.1 | async-start | bytes 2367488 | tf_op jit(solution)/shard_map/reduce_scatter | solution.py:176
  7.2 12.9 %collective-permute-start = (bf16[256,132]{0,1:T(8,128)(2,1)}, bf16[256,132]{0,1:T(8,128)(2,1)S(1)}, u32[]{:S(2)}, u32[]{:S(2)}) collective-permute-start(bf16[256,132]{0,1:T(8,128)(2,1)} %param.15), channel_id=1, source_target_pairs={{0,2},{2,4},{4,6},{6,8},{8,10},{10,12},{12,14},{14,16},{16,18},{18... | collective-permute-start | bytes 202760 | tf_op jit(solution)/shard_map/ppermute | solution.py:152
  10.2 9.9 %collective-permute-start.1 = (bf16[256,132]{0,1:T(8,128)(2,1)}, bf16[256,132]{0,1:T(8,128)(2,1)S(1)}, u32[]{:S(2)}, u32[]{:S(2)}) collective-permute-start(bf16[256,132]{0,1:T(8,128)(2,1)} %param.15), channel_id=1, source_target_pairs={{0,30},{2,0},{4,2},{6,4},{8,6},{10,8},{12,10},{14,12},{16,14},{18,... | collective-permute-start | bytes 202760 | tf_op jit(solution)/shard_map/ppermute | solution.py:158
  14.9 61.6 %copy-start.23 = (f32[68]{0:T(128)}, f32[68]{0:T(128)S(1)}, u32[]{:S(2)}) copy-start(f32[68]{0:T(128)S(1)} %exponential_negate_fusion) | copy-start | bytes 820
  14.9 2.5 %copy-start.7 = (bf16[1,128,64]{1,2,0:T(8,128)(2,1)S(1)}, bf16[1,128,64]{1,2,0:T(8,128)(2,1)}, u32[]{:S(2)}) copy-start(bf16[1,128,64]{1,2,0:T(8,128)(2,1)} %param.14) | copy-start | bytes 49156
  16.3 62.6 %copy-start.6 = (bf16[1,128,2176]{1,2,0:T(8,128)(2,1)}, bf16[1,128,2176]{1,2,0:T(8,128)(2,1)S(1)}, u32[]{:S(2)}) copy-start(bf16[1,128,2176]{1,2,0:T(8,128)(2,1)S(1)} %copy.78) | copy-start | bytes 1671172
  20.1 8.0 %collective-permute-start.2 = (bf16[256,132]{0,1:T(8,128)(2,1)S(1)}, bf16[256,132]{0,1:T(8,128)(2,1)S(1)}, u32[]{:S(2)}, u32[]{:S(2)}) collective-permute-start(bf16[256,132]{0,1:T(8,128)(2,1)S(1)} %collective-permute-done), channel_id=1, source_target_pairs={{0,2},{2,4},{4,6},{6,8},{8,10},{10,12},{12,14},{14,16},{16,18},{18... | collective-permute-start | bytes 202760 | tf_op jit(solution)/shard_map/ppermute | solution.py:152
  20.2 8.0 %collective-permute-start.3 = (bf16[256,132]{0,1:T(8,128)(2,1)S(1)}, bf16[256,132]{0,1:T(8,128)(2,1)S(1)}, u32[]{:S(2)}, u32[]{:S(2)}) collective-permute-start(bf16[256,132]{0,1:T(8,128)(2,1)S(1)} %collective-permute-done.1), channel_id=1, source_target_pairs={{0,30},{2,0},{4,2},{6,4},{8,6},{10,8},{12,10},{14,12},{16,14},{18,... | collective-permute-start | bytes 202760 | tf_op jit(solution)/shard_map/ppermute | solution.py:158
  28.2 7.9 %collective-permute-start.4 = (bf16[256,132]{0,1:T(8,128)(2,1)S(1)}, bf16[256,132]{0,1:T(8,128)(2,1)S(1)}, u32[]{:S(2)}, u32[]{:S(2)}) collective-permute-start(bf16[256,132]{0,1:T(8,128)(2,1)S(1)} %collective-permute-done.2), channel_id=1, source_target_pairs={{0,2},{2,4},{4,6},{6,8},{8,10},{10,12},{12,14},{14,16},{16,18},{18... | collective-permute-start | bytes 202760 | tf_op jit(solution)/shard_map/ppermute | solution.py:152
  28.2 7.9 %collective-permute-start.5 = (bf16[256,132]{0,1:T(8,128)(2,1)S(1)}, bf16[256,132]{0,1:T(8,128)(2,1)S(1)}, u32[]{:S(2)}, u32[]{:S(2)}) collective-permute-start(bf16[256,132]{0,1:T(8,128)(2,1)S(1)} %collective-permute-done.3), channel_id=1, source_target_pairs={{0,30},{2,0},{4,2},{6,4},{8,6},{10,8},{12,10},{14,12},{16,14},{18,... | collective-permute-start | bytes 202760 | tf_op jit(solution)/shard_map/ppermute | solution.py:158
  36.1 8.0 %collective-permute-start.6 = (bf16[256,132]{0,1:T(8,128)(2,1)S(1)}, bf16[256,132]{0,1:T(8,128)(2,1)S(1)}, u32[]{:S(2)}, u32[]{:S(2)}) collective-permute-start(bf16[256,132]{0,1:T(8,128)(2,1)S(1)} %collective-permute-done.4), channel_id=1, source_target_pairs={{0,2},{2,4},{4,6},{6,8},{8,10},{10,12},{12,14},{14,16},{16,18},{18... | collective-permute-start | bytes 202760 | tf_op jit(solution)/shard_map/ppermute | solution.py:152
  36.1 8.0 %collective-permute-start.7 = (bf16[256,132]{0,1:T(8,128)(2,1)S(1)}, bf16[256,132]{0,1:T(8,128)(2,1)S(1)}, u32[]{:S(2)}, u32[]{:S(2)}) collective-permute-start(bf16[256,132]{0,1:T(8,128)(2,1)S(1)} %collective-permute-done.5), channel_id=1, source_target_pairs={{0,30},{2,0},{4,2},{6,4},{8,6},{10,8},{12,10},{14,12},{16,14},{18,... | collective-permute-start | bytes 202760 | tf_op jit(solution)/shard_map/ppermute | solution.py:158
  44.1 7.9 %collective-permute-start.8 = (bf16[256,132]{0,1:T(8,128)(2,1)S(1)}, bf16[256,132]{0,1:T(8,128)(2,1)S(1)}, u32[]{:S(2)}, u32[]{:S(2)}) collective-permute-start(bf16[256,132]{0,1:T(8,128)(2,1)S(1)} %collective-permute-done.6), channel_id=1, source_target_pairs={{0,2},{2,4},{4,6},{6,8},{8,10},{10,12},{12,14},{14,16},{16,18},{18... | collective-permute-start | bytes 202760 | tf_op jit(solution)/shard_map/ppermute | solution.py:152
  44.1 7.9 %collective-permute-start.9 = (bf16[256,132]{0,1:T(8,128)(2,1)S(1)}, bf16[256,132]{0,1:T(8,128)(2,1)S(1)}, u32[]{:S(2)}, u32[]{:S(2)}) collective-permute-start(bf16[256,132]{0,1:T(8,128)(2,1)S(1)} %collective-permute-done.7), channel_id=1, source_target_pairs={{0,30},{2,0},{4,2},{6,4},{8,6},{10,8},{12,10},{14,12},{16,14},{18,... | collective-permute-start | bytes 202760 | tf_op jit(solution)/shard_map/ppermute | solution.py:158
  52.0 8.1 %collective-permute-start.10 = (bf16[256,132]{0,1:T(8,128)(2,1)S(1)}, bf16[256,132]{0,1:T(8,128)(2,1)S(1)}, u32[]{:S(2)}, u32[]{:S(2)}) collective-permute-start(bf16[256,132]{0,1:T(8,128)(2,1)S(1)} %collective-permute-done.8), channel_id=1, source_target_pairs={{0,2},{2,4},{4,6},{6,8},{8,10},{10,12},{12,14},{14,16},{16,18},{18... | collective-permute-start | bytes 202760 | tf_op jit(solution)/shard_map/ppermute | solution.py:152
  52.0 8.1 %collective-permute-start.11 = (bf16[256,132]{0,1:T(8,128)(2,1)S(1)}, bf16[256,132]{0,1:T(8,128)(2,1)S(1)}, u32[]{:S(2)}, u32[]{:S(2)}) collective-permute-start(bf16[256,132]{0,1:T(8,128)(2,1)S(1)} %collective-permute-done.9), channel_id=1, source_target_pairs={{0,30},{2,0},{4,2},{6,4},{8,6},{10,8},{12,10},{14,12},{16,14},{18,... | collective-permute-start | bytes 202760 | tf_op jit(solution)/shard_map/ppermute | solution.py:158
  60.0 8.1 %collective-permute-start.12 = (bf16[256,132]{0,1:T(8,128)(2,1)S(1)}, bf16[256,132]{0,1:T(8,128)(2,1)S(1)}, u32[]{:S(2)}, u32[]{:S(2)}) collective-permute-start(bf16[256,132]{0,1:T(8,128)(2,1)S(1)} %collective-permute-done.10), channel_id=1, source_target_pairs={{0,2},{2,4},{4,6},{6,8},{8,10},{10,12},{12,14},{14,16},{16,18},{18... | collective-permute-start | bytes 202760 | tf_op jit(solution)/shard_map/ppermute | solution.py:152
  60.1 8.1 %collective-permute-start.13 = (bf16[256,132]{0,1:T(8,128)(2,1)S(1)}, bf16[256,132]{0,1:T(8,128)(2,1)S(1)}, u32[]{:S(2)}, u32[]{:S(2)}) collective-permute-start(bf16[256,132]{0,1:T(8,128)(2,1)S(1)} %collective-permute-done.11), channel_id=1, source_target_pairs={{0,30},{2,0},{4,2},{6,4},{8,6},{10,8},{12,10},{14,12},{16,14},{18,... | collective-permute-start | bytes 202760 | tf_op jit(solution)/shard_map/ppermute | solution.py:158
  68.2 7.9 %collective-permute-start.14 = (bf16[256,132]{0,1:T(8,128)(2,1)S(1)}, bf16[256,132]{0,1:T(8,128)(2,1)S(1)}, u32[]{:S(2)}, u32[]{:S(2)}) collective-permute-start(bf16[256,132]{0,1:T(8,128)(2,1)S(1)} %collective-permute-done.12), channel_id=1, source_target_pairs={{0,2},{2,4},{4,6},{6,8},{8,10},{10,12},{12,14},{14,16},{16,18},{18... | collective-permute-start | bytes 202760 | tf_op jit(solution)/shard_map/ppermute | solution.py:152
  88.3 3.6 %copy-start.26 = (bf16[2,68]{1,0:T(2,128)(2,1)S(1)}, bf16[2,68]{1,0:T(2,128)(2,1)}, u32[]{:S(2)}) copy-start(bf16[2,68]{1,0:T(2,128)(2,1)} %get-tuple-element.716) | copy-start | bytes 820
  132.1 2.0 copy-start.16
  132.1 2.8 %copy-start.2 = (bf16[1,128,2176]{1,2,0:T(8,128)(2,1)S(1)}, bf16[1,128,2176]{1,2,0:T(8,128)(2,1)}, u32[]{:S(2)}) copy-start(bf16[1,128,2176]{1,2,0:T(8,128)(2,1)} %copy.65) | copy-start | bytes 1671172
  132.1 2.8 %copy-start.10 = (f32[1,68,128]{2,1,0:T(8,128)S(1)}, f32[1,68,128]{2,1,0:T(8,128)}, u32[]{:S(2)}) copy-start(f32[1,68,128]{2,1,0:T(8,128)} %copy-done.9) | copy-start | bytes 104452
  132.2 2.8 %copy-start.18 = (f32[128,128]{1,0:T(8,128)S(1)}, f32[128,128]{1,0:T(8,128)}, u32[]{:S(2)}) copy-start(f32[128,128]{1,0:T(8,128)} %copy.72) | copy-start | bytes 196612
  132.2 2.8 %copy-start.19 = (f32[68,128]{1,0:T(8,128)S(1)}, f32[68,128]{1,0:T(8,128)}, u32[]{:S(2)}) copy-start(f32[68,128]{1,0:T(8,128)} %copy.75) | copy-start | bytes 104452
  132.2 2.8 %copy-start.20 = (pred[128,128]{1,0:T(8,128)(4,1)S(1)}, pred[128,128]{1,0:T(8,128)(4,1)}, u32[]{:S(2)}) copy-start(pred[128,128]{1,0:T(8,128)(4,1)} %iota_compare_fusion) | copy-start | bytes 49156
  135.0 2.0 copy-start.13
  135.0 2.0 copy-start.15
  137.0 75.6 %copy-start.4 = (f32[128,68]{1,0:T(8,128)S(1)}, f32[128,68]{1,0:T(8,128)}, u32[]{:S(2)}) copy-start(f32[128,68]{1,0:T(8,128)} %copy-done.3) | copy-start | bytes 104452
  210.3 4.2 %collective-permute-start.15 = (f32[256,6]{0,1:T(8,128)S(1)}, f32[256,6]{0,1:T(8,128)S(1)}, u32[]{:S(2)}, u32[]{:S(2)}) collective-permute-start(f32[256,6]{0,1:T(8,128)S(1)} %slice.28), channel_id=1, source_target_pairs={{0,1},{2,3},{4,5},{6,7},{8,9},{10,11},{12,13},{14,15},{16,17},{18,... | collective-permute-start | bytes 18440
  (12 other events, 13.3 us)
Sparse Core Ops, SparseCore 0:
  129.6 77.0 reduce-scatter.3
